TPU v7x, 128 devices: a whole 4x4x4 slice. The times are simulated.
128 devices in a mesh: ent: 32 (over x, z, y_lo), qry: 4 (over y_hi, core).
Axes of the slice: x: 4, y: 4 (y_hi: 2, y_lo: 2; y = y_hi * 2 + y_lo), z: 4, core: 2. Of those that a mesh axis runs over, the one named last changes fastest.
Arguments:
- ent_emb: bfloat16 [65536, 512], P('ent'), may hold values from -1 to 1
- ent_tan: bfloat16 [65536, 512], P('ent'), may hold values from -0.25 to 0.25
- qry_emb: bfloat16 [4096, 512], P(('qry', 'ent')), may hold values from -6 to 6
- qry_tan: bfloat16 [4096, 512], P(('qry', 'ent')), may hold values from -6 to 6
- tails: int32 [4096, 4], P('qry'), may hold values from 0 to 65535
Outputs:
- ent_gnvp: float32 [65536, 512], P(('ent', 'qry'))
- ent_grad: float32 [65536, 512], P(('ent', 'qry'))
- qry_gnvp: float32 [4096, 512], P(('qry', 'ent'))
- qry_grad: float32 [4096, 512], P(('qry', 'ent'))
All inputs are finite; a program needn't handle non-finite values.
Results may differ from a plain program's by a relative error of at most 0.0008.
Values may be sent and summed in bfloat16 or wider, within the bound.
A program may use at most 128 MiB of HBM per device.

v0:
```python
import jax
import jax.numpy as jnp
from jax import lax
from jax.sharding import PartitionSpec as P


def dot_nt(a, b):
    return lax.dot_general(a, b, (((1,), (1,)), ((), ())), preferred_element_type=jnp.float32)


def dot_tn(a, b):
    return lax.dot_general(a, b, (((0,), (0,)), ((), ())), preferred_element_type=jnp.float32)


def weights(queries, qtangent, tail_rows, entities, etangent, ent_ids):
    score = dot_nt(queries, entities)
    dscore = dot_nt(qtangent, entities) + dot_nt(queries, etangent)
    prob = jax.nn.sigmoid(score)
    label = jnp.zeros(score.shape, jnp.float32)
    for k in range(tail_rows.shape[1]):
        label = jnp.maximum(
            label, (tail_rows[:, k : k + 1] == ent_ids[None, :]).astype(jnp.float32)
        )
    ugrad = (prob - label).astype(jnp.bfloat16)
    uhess = (prob * (1.0 - prob) * dscore).astype(jnp.bfloat16)
    return (uhess, ugrad)


def per_device(ent_emb, ent_tan, qry_emb, qry_tan, tails):
    ent_rows = ent_emb.shape[0]
    width = ent_emb.shape[1]
    panel_q, panel_dq = (
        lax.all_gather(qry_emb, "ent", axis=0, tiled=True),
        lax.all_gather(qry_tan, "ent", axis=0, tiled=True),
    )
    entities, etangent = (ent_emb, ent_tan)
    ent_ids = lax.axis_index("ent") * ent_rows + jnp.arange(ent_rows, dtype=jnp.int32)
    queries, qtangent, tail_rows = (panel_q, panel_dq, tails)
    uhess, ugrad = weights(queries, qtangent, tail_rows, entities, etangent, ent_ids)
    qrows = lax.psum_scatter(
        jnp.concatenate(
            [
                jnp.dot(uhess, entities, preferred_element_type=jnp.float32),
                jnp.dot(ugrad, entities, preferred_element_type=jnp.float32),
            ],
            axis=1,
        ),
        "ent",
        scatter_dimension=0,
        tiled=True,
    )
    erows = lax.psum_scatter(
        jnp.concatenate([dot_tn(uhess, queries), dot_tn(ugrad, queries)], axis=1),
        "qry",
        scatter_dimension=0,
        tiled=True,
    )
    return (erows[:, :width], erows[:, width:], qrows[:, :width], qrows[:, width:])


def solution(mesh):
    return jax.shard_map(
        per_device,
        mesh=mesh,
        in_specs=(
            P("ent", None),
            P("ent", None),
            P(("qry", "ent"), None),
            P(("qry", "ent"), None),
            P("qry", None),
        ),
        out_specs=(
            P(("ent", "qry"), None),
            P(("ent", "qry"), None),
            P(("qry", "ent"), None),
            P(("qry", "ent"), None),
        ),
        check_vma=False,
    )
```

profile of v0, /device:TPU:1, one launch (start us, length us, event | category | flops | bytes accessed | tf_op | source)
XLA Modules:
  0.0 606.4 jit_solution(13524694855700156160)
XLA Ops:
  7.2 0.0 copy-start
  7.2 0.0 all-gather.5.cloned.1.call-start
  7.2 0.7 all-gather.5.cloned.1.call-update
  7.9 0.0 all-gather.3.cloned.1.call-start
  8.0 0.7 all-gather.3.cloned.1.call-update
  8.7 0.0 reduce-scatter.7.cloned.1.call-start
  8.7 0.9 fusion.4
  9.6 132.4 %all-gather.5.cloned.1.call-done = bf16[1024,512]{1,0:T(8,128)(2,1)} async-done(((bf16[32,512]{1,0:T(8,128)(2,1)}), bf16[1024,512]{1,0:T(8,128)(2,1)}) %all-gather.5.cloned.1.call-update) | async-done | bytes 1048592 | tf_op jit(solution)/shard_map/all_gather | solution.py:34
  142.0 0.0 copy-done
  142.0 6.8 %fusion.5 = f32[1024,2048]{1,0:T(8,128)} fusion(bf16[1024,512]{1,0:T(8,128)(2,1)} %all-gather.5.cloned.1.call-done, bf16[2048,512]{1,0:T(8,128)(2,1)S(1)} %copy-done), kind=kOutput, calls=%fused_computation.11 | convolution fusion | flops 2147483648 | bytes 11534336 | tf_op jit(solution)/shard_map/dot_general | solution.py:8
  148.8 145.9 %all-gather.3.cloned.1.call-done = bf16[1024,512]{1,0:T(8,128)(2,1)} async-done(((bf16[32,512]{1,0:T(8,128)(2,1)}), bf16[1024,512]{1,0:T(8,128)(2,1)}) %all-gather.3.cloned.1.call-update) | async-done | bytes 1048592 | tf_op jit(solution)/shard_map/all_gather | solution.py:33
  294.7 0.0 copy-start.2
  294.7 8.4 %subtract_convert_fusion = (bf16[1024,2048]{1,0:T(8,128)(2,1)}, f32[1024,2048]{1,0:T(8,128)S(1)}) fusion(s32[2048]{0:T(1024)S(1)} %iota_add_fusion, s32[1024]{0:T(1024)S(1)} %bitcast.21, s32[1024]{0:T(1024)S(1)} %bitcast.22, s32[1024]{0:T(1024)S(1)} %bitcast.20, s32[1024]{0:T(1024)S(1)} %bitcast.19, bf16[1024,512]{1,0:T(8,128)(2,1)} %all-gather.3.cloned.1.call-done, ...), kind=kOutput, calls=%fused_computation.4 | convolution fusion | flops 2183135232 | bytes 15753216 | tf_op jit(solution)/shard_map/dot_general | solution.py:8
  303.1 0.0 copy-done.2
  303.1 6.5 %fusion.1 = bf16[1024,2048]{1,0:T(8,128)(2,1)} fusion(f32[1024,2048]{1,0:T(8,128)S(1)} %get-tuple-element.21, f32[1024,2048]{1,0:T(8,128)S(1)} %copy-done.2, bf16[1024,512]{1,0:T(8,128)(2,1)} %all-gather.3.cloned.1.call-done, bf16[2048,512]{1,0:T(8,128)(2,1)} %param.6), kind=kOutput, calls=%fused_computation.2 | convolution fusion | flops 2157969408 | bytes 24117248 | tf_op jit(solution)/shard_map/dot_general | solution.py:8
  309.6 0.0 copy-start.4
  309.7 4.7 fusion.8
  314.4 0.0 copy-done.4
  314.4 2.4 fusion.9
  316.8 2.5 pad_maximum_fusion.1
  319.3 5.4 copy.17
  324.7 0.0 copy-start.3
  324.7 0.0 reduce-scatter.7.cloned.1.call-update
  324.7 0.2 reduce-scatter.5.cloned.1.call-start
  324.9 1.0 copy-done.3
  325.9 0.0 copy-start.5
  325.9 4.7 fusion.6
  330.6 0.0 copy-done.5
  330.6 2.5 fusion.7
  333.1 3.8 pad_maximum_fusion
  336.9 0.0 reduce-scatter.5.cloned.1.call-update
  337.0 155.2 %reduce-scatter.7.cloned.1.call-done = f32[32,1024]{1,0:T(8,128)} async-done(((f32[1024,1024]{1,0:T(8,128)}), f32[32,1024]{1,0:T(8,128)}) %reduce-scatter.7.cloned.1.call-update) | async-done | bytes 131088
  492.2 0.0 copy-start.1
  492.2 1.7 fusion.3
  493.9 99.5 %reduce-scatter.5.cloned.1.call-done = f32[512,1024]{0,1:T(8,128)} async-done(((f32[2048,1024]{0,1:T(8,128)}), f32[512,1024]{0,1:T(8,128)}) %reduce-scatter.5.cloned.1.call-update) | async-done | bytes 2097168 | tf_op jit(solution)/shard_map/reduce_scatter | solution.py:52
  593.3 2.7 fusion.2
  596.0 2.5 copy.14
  598.5 1.3 copy.13
  599.8 0.0 copy-done.1
  (1 shorter events, 0.0 us)
Async XLA Ops:
  7.2 134.8 %copy-start = (bf16[2048,512]{1,0:T(8,128)(2,1)S(1)}, bf16[2048,512]{1,0:T(8,128)(2,1)}, u32[]{:S(2)}) copy-start(bf16[2048,512]{1,0:T(8,128)(2,1)} %param.5) | copy-start | bytes 6291460
  7.2 134.8 %all-gather.5.cloned.1.call-start = ((), (), s32[]{:S(2)}) async-start(), calls=%async_computation.3 | async-start | bytes 1081344 | tf_op jit(solution)/shard_map/all_gather | solution.py:34
  7.9 286.8 %all-gather.3.cloned.1.call-start = ((), (), s32[]{:S(2)}) async-start(), calls=%async_computation.2 | async-start | bytes 1081344 | tf_op jit(solution)/shard_map/all_gather | solution.py:33
  8.7 483.5 %reduce-scatter.7.cloned.1.call-start = ((), (), s32[]{:S(2)}) async-start(), calls=%async_computation.5 | async-start | bytes 4325376
  294.7 8.4 %copy-start.2 = (f32[1024,2048]{1,0:T(8,128)S(1)}, f32[1024,2048]{1,0:T(8,128)}, u32[]{:S(2)}) copy-start(f32[1024,2048]{1,0:T(8,128)} %fusion.5) | copy-start | bytes 25165828
  309.6 4.7 copy-start.4
  324.7 1.2 copy-start.3
  324.7 268.6 %reduce-scatter.5.cloned.1.call-start = ((), (), s32[]{:S(2)}) async-start(), calls=%async_computation.4 | async-start | bytes 10485760 | tf_op jit(solution)/shard_map/reduce_scatter | solution.py:52
  325.9 4.7 copy-start.5
  492.2 107.7 %copy-start.1 = (bf16[2048,512]{1,0:T(8,128)(2,1)S(1)}, bf16[2048,512]{1,0:T(8,128)(2,1)}, u32[]{:S(2)}) copy-start(bf16[2048,512]{1,0:T(8,128)(2,1)} %param.5) | copy-start | bytes 6291460
Sparse Core Ops, SparseCore 0:
  9.7 132.2 all-gather.4
  143.6 151.0 all-gather.2
  324.8 167.3 reduce-scatter.6
  494.7 98.5 reduce-scatter.4
where the time goes:
time: 607 us; the launch traced here: 606 us
  waiting for transfers between devices  534 us (88%)
  matrix products  36.1 us (6%)
  local copies, waits for them, and re-layouts  15.4 us (3%)
  between operations  13.8 us (2%)
  other arithmetic  6.33 us (1%)
    unnamed x5, waiting for transfers between devices  157 us
    all_gather x1, waiting for transfers between devices, per_device(): lax.all_gather(qry_emb, 'ent', axis=0, tiled=True)  146 us
    all_gather x1, waiting for transfers between devices, per_device(): lax.all_gather(qry_tan, 'ent', axis=0, tiled=True)  132 us
    reduce_scatter x1, waiting for transfers between devices, per_device(): lax.psum_scatter(jnp.concatenate([dot_tn(uhess, queries), dot_tn(ugrad, q...  99.5 us
    dot_general x3, matrix products, dot_nt(): lax.dot_general(a, b, (((1,), (1,)), ((), ())), preferred_element_type=jn...  21.7 us
  transfers between devices with their start and end apart: 4, of which 4 were waited for; matrix products, arithmetic and copies ran while one was open for 3% of the time, Pallas kernels for 0%

commit v1 on v0

--- a/solution.py
+++ b/solution.py
@@ -31,7 +31,9 @@
     width = ent_emb.shape[1]
     panel_q, panel_dq = (
         lax.all_gather(qry_emb, "ent", axis=0, tiled=True),
-        lax.all_gather(qry_tan, "ent", axis=0, tiled=True),
+        jnp.concatenate(
+            lax.all_to_all(jnp.stack([qry_tan] * lax.axis_size("ent")), "ent", 0, 0), axis=0
+        ),
     )
     entities, etangent = (ent_emb, ent_tan)
     ent_ids = lax.axis_index("ent") * ent_rows + jnp.arange(ent_rows, dtype=jnp.int32)

time: 607 us -> 458 us (0.75)
  waiting for transfers between devices: 534 us -> 376 us
  starting transfers between devices: 0.34 us -> 10 us
    all_gather x1 -> x0, waiting for transfers between devices: 132 us -> none  [per_device(): lax.all_gather(qry_tan, 'ent', axis=0, tiled=True)]
    all_gather x1, waiting for transfers between devices: 146 us -> 106 us  [per_device(): lax.all_gather(qry_emb, 'ent', axis=0, tiled=True)]
    all_to_all x0 -> x1, waiting for transfers between devices: none -> 15.4 us  [per_device(): lax.all_to_all(jnp.stack([qry_tan] * lax.axis_size('ent')), 'ent', 0, 0)]
    all_to_all x0 -> x1, starting transfers between devices: none -> 9.73 us  [per_device(): lax.all_to_all(jnp.stack([qry_tan] * lax.axis_size('ent')), 'ent', 0, 0)]
    unnamed x5 -> x4, waiting for transfers between devices: 157 us -> 155 us
  transfers between devices with their start and end apart: 4 -> 4, of which waited for: 4 -> 4; matrix products, arithmetic and copies ran while one was open for 3% -> 5% of each run, Pallas kernels for 0% -> 0%
where the time goes in v1:
time: 458 us
  waiting for transfers between devices  376 us (82%)
  matrix products  34.8 us (8%)
  local copies, waits for them, and re-layouts  17.1 us (4%)
  between operations  13.8 us (3%)
  starting transfers between devices  10 us (2%)
  other arithmetic  6.31 us (1%)
    unnamed x4, waiting for transfers between devices  155 us
    all_gather x1, waiting for transfers between devices, per_device(): lax.all_gather(qry_emb, 'ent', axis=0, tiled=True)  106 us
    reduce_scatter x1, waiting for transfers between devices, per_device(): lax.psum_scatter(jnp.concatenate([dot_tn(uhess, queries), dot_tn(ugrad, q...  99.9 us
    dot_general x3, matrix products, dot_nt(): lax.dot_general(a, b, (((1,), (1,)), ((), ())), preferred_element_type=jn...  20.5 us
    all_to_all x1, waiting for transfers between devices, per_device(): lax.all_to_all(jnp.stack([qry_tan] * lax.axis_size('ent')), 'ent', 0, 0)  15.4 us
    unnamed x13, local copies, waits for them, and re-layouts  10.2 us
    all_to_all x1, starting transfers between devices, per_device(): lax.all_to_all(jnp.stack([qry_tan] * lax.axis_size('ent')), 'ent', 0, 0)  9.73 us
  transfers between devices with their start and end apart: 4, of which 4 were waited for; matrix products, arithmetic and copies ran while one was open for 5% of the time, Pallas kernels for 0%

profile of v1, /device:TPU:1, one launch (start us, length us, event | category | flops | bytes accessed | tf_op | source)
XLA Modules:
  0.0 457.7 jit_solution(6288747668821374540)
XLA Ops:
  7.2 0.0 copy-start
  7.2 0.0 all-gather.2.cloned.1.call-start
  7.2 0.7 all-gather.2.cloned.1.call-update
  7.9 1.8 stack.2
  9.8 9.7 %all-to-all-start = ((bf16[32,32,512]{2,1,0:T(8,128)(2,1)}), bf16[32,32,512]{2,1,0:T(8,128)(2,1)S(1)}, u32[]{:S(2)}, u32[]{:S(2)}) async-start(bf16[32,32,512]{2,1,0:T(8,128)(2,1)} %stack.2), calls=%async_computation | async-start | bytes 2097152 | tf_op jit(solution)/shard_map/all_to_all | solution.py:35
  19.5 0.0 reduce-scatter.7.cloned.1.call-start
  19.6 0.9 fusion.4
  20.5 15.4 %all-to-all-done = bf16[32,32,512]{2,1,0:T(8,128)(2,1)S(1)} async-done(((bf16[32,32,512]{2,1,0:T(8,128)(2,1)}), bf16[32,32,512]{2,1,0:T(8,128)(2,1)S(1)}, u32[]{:S(2)}, u32[]{:S(2)}) %all-to-all-start) | async-done | bytes 1048608 | tf_op jit(solution)/shard_map/all_to_all | solution.py:35
  35.8 0.0 copy-done
  35.8 5.6 %fusion.5 = f32[1024,2048]{1,0:T(8,128)} fusion(bf16[1024,512]{1,0:T(8,128)(2,1)S(1)} %bitcast.20, bf16[2048,512]{1,0:T(8,128)(2,1)S(1)} %copy-done), kind=kOutput, calls=%fused_computation.11 | convolution fusion | flops 2147483648 | bytes 11534336 | tf_op jit(solution)/shard_map/dot_general | solution.py:8
  41.4 105.5 %all-gather.2.cloned.1.call-done = bf16[1024,512]{1,0:T(8,128)(2,1)} async-done(((bf16[32,512]{1,0:T(8,128)(2,1)}), bf16[1024,512]{1,0:T(8,128)(2,1)}) %all-gather.2.cloned.1.call-update) | async-done | bytes 1048592 | tf_op jit(solution)/shard_map/all_gather | solution.py:33
  147.0 0.0 copy-start.1
  147.0 8.4 %subtract_convert_fusion = (bf16[1024,2048]{1,0:T(8,128)(2,1)}, f32[1024,2048]{1,0:T(8,128)S(1)}) fusion(s32[2048]{0:T(1024)S(1)} %iota_add_fusion, s32[1024]{0:T(1024)S(1)} %bitcast.23, s32[1024]{0:T(1024)S(1)} %bitcast.24, s32[1024]{0:T(1024)S(1)} %bitcast.22, s32[1024]{0:T(1024)S(1)} %bitcast.21, bf16[1024,512]{1,0:T(8,128)(2,1)} %all-gather.2.cloned.1.call-done, ...), kind=kOutput, calls=%fused_computation.4 | convolution fusion | flops 2183135232 | bytes 15753216 | tf_op jit(solution)/shard_map/dot_general | solution.py:8
  155.3 0.0 copy-done.1
  155.3 6.5 %fusion.1 = bf16[1024,2048]{1,0:T(8,128)(2,1)} fusion(f32[1024,2048]{1,0:T(8,128)S(1)} %get-tuple-element.21, f32[1024,2048]{1,0:T(8,128)S(1)} %copy-done.1, bf16[1024,512]{1,0:T(8,128)(2,1)} %all-gather.2.cloned.1.call-done, bf16[2048,512]{1,0:T(8,128)(2,1)} %param.6), kind=kOutput, calls=%fused_computation.2 | convolution fusion | flops 2157969408 | bytes 24117248 | tf_op jit(solution)/shard_map/dot_general | solution.py:8
  161.8 0.0 copy-start.3
  161.8 4.7 %fusion.8 = f32[1024,512]{0,1:T(8,128)S(1)} fusion(bf16[1024,2048]{1,0:T(8,128)(2,1)} %fusion.1, bf16[2048,512]{1,0:T(8,128)(2,1)S(1)} %copy-done), kind=kOutput, calls=%fused_computation.14 | convolution fusion | flops 2147483648 | bytes 8388608 | tf_op jit(solution)/shard_map/dot_general | solution.py:45
  166.5 0.0 copy-done.3
  166.6 2.4 fusion.9
  169.0 2.5 pad_maximum_fusion.1
  171.5 5.3 %copy.17 = f32[1024,1024]{1,0:T(8,128)} copy(f32[1024,1024]{0,1:T(8,128)} %pad_maximum_fusion.1) | data formatting | bytes 8388608
  176.8 0.0 copy-start.2
  176.8 0.0 reduce-scatter.7.cloned.1.call-update
  176.9 0.2 reduce-scatter.5.cloned.1.call-start
  177.1 1.0 copy-done.2
  178.1 0.0 copy-start.4
  178.1 4.7 %fusion.6 = f32[2048,512]{0,1:T(8,128)S(1)} fusion(bf16[1024,2048]{1,0:T(8,128)(2,1)} %fusion.1, bf16[1024,512]{1,0:T(8,128)(2,1)S(1)} %copy-done.2), kind=kOutput, calls=%fused_computation.12 | convolution fusion | flops 2147483648 | bytes 9437184 | tf_op jit(solution)/shard_map/dot_general | solution.py:12
  182.8 0.0 copy-done.4
  182.8 2.5 fusion.7
  185.3 3.8 pad_maximum_fusion
  189.1 0.0 reduce-scatter.5.cloned.1.call-update
  189.1 154.1 %reduce-scatter.7.cloned.1.call-done = f32[32,1024]{1,0:T(8,128)} async-done(((f32[1024,1024]{1,0:T(8,128)}), f32[32,1024]{1,0:T(8,128)}) %reduce-scatter.7.cloned.1.call-update) | async-done | bytes 131088
  343.2 1.5 fusion.3
  344.7 99.9 %reduce-scatter.5.cloned.1.call-done = f32[512,1024]{0,1:T(8,128)} async-done(((f32[2048,1024]{0,1:T(8,128)}), f32[512,1024]{0,1:T(8,128)}) %reduce-scatter.5.cloned.1.call-update) | async-done | bytes 2097168 | tf_op jit(solution)/shard_map/reduce_scatter | solution.py:54
  444.7 2.7 fusion.2
  447.3 2.5 copy.14
  449.9 1.3 copy.13
  (1 shorter events, 0.0 us)
Async XLA Ops:
  7.2 28.7 %copy-start = (bf16[2048,512]{1,0:T(8,128)(2,1)S(1)}, bf16[2048,512]{1,0:T(8,128)(2,1)}, u32[]{:S(2)}) copy-start(bf16[2048,512]{1,0:T(8,128)(2,1)} %param.5) | copy-start | bytes 6291460
  7.2 139.8 %all-gather.2.cloned.1.call-start = ((), (), s32[]{:S(2)}) async-start(), calls=%async_computation.3 | async-start | bytes 1081344 | tf_op jit(solution)/shard_map/all_gather | solution.py:33
  9.8 26.1 %all-to-all-start = ((bf16[32,32,512]{2,1,0:T(8,128)(2,1)}), bf16[32,32,512]{2,1,0:T(8,128)(2,1)S(1)}, u32[]{:S(2)}, u32[]{:S(2)}) async-start(bf16[32,32,512]{2,1,0:T(8,128)(2,1)} %stack.2), calls=%async_computation | async-start | bytes 2097152 | tf_op jit(solution)/shard_map/all_to_all | solution.py:35
  19.5 323.7 %reduce-scatter.7.cloned.1.call-start = ((), (), s32[]{:S(2)}) async-start(), calls=%async_computation.5 | async-start | bytes 4325376
  147.0 8.4 %copy-start.1 = (f32[1024,2048]{1,0:T(8,128)S(1)}, f32[1024,2048]{1,0:T(8,128)}, u32[]{:S(2)}) copy-start(f32[1024,2048]{1,0:T(8,128)} %fusion.5) | copy-start | bytes 25165828
  161.8 4.7 %copy-start.3 = (bf16[1024,2048]{1,0:T(8,128)(2,1)S(1)}, bf16[1024,2048]{1,0:T(8,128)(2,1)}, u32[]{:S(2)}) copy-start(bf16[1024,2048]{1,0:T(8,128)(2,1)} %get-tuple-element.20) | copy-start | bytes 12582916
  176.8 1.2 copy-start.2
  176.9 267.8 %reduce-scatter.5.cloned.1.call-start = ((), (), s32[]{:S(2)}) async-start(), calls=%async_computation.4 | async-start | bytes 10485760 | tf_op jit(solution)/shard_map/reduce_scatter | solution.py:54
  178.1 4.7 %copy-start.4 = (bf16[1024,2048]{1,0:T(8,128)(2,1)S(1)}, bf16[1024,2048]{1,0:T(8,128)(2,1)}, u32[]{:S(2)}) copy-start(bf16[1024,2048]{1,0:T(8,128)(2,1)} %get-tuple-element.20) | copy-start | bytes 12582916
Sparse Core Ops, SparseCore 0:
  9.7 137.2 all-gather.1
  177.0 166.1 reduce-scatter.6
  345.9 98.7 reduce-scatter.4
